TPU v7x, 32 devices: a whole 2x2x4 slice. The times are simulated.
32 devices in a mesh: clip: 16 (over z, x, core), frame: 2 (over y).
Axes of the slice: x: 2, y: 2, z: 4, core: 2. Of those that a mesh axis runs over, the one named last changes fastest.
Arguments:
- inputs: bfloat16 [16, 1500, 768], P('clip', 'frame'), may hold values from -6 to 6
- cotangent: bfloat16 [16, 1500, 768], P('clip', 'frame'), may hold values from -2 to 2
- project_in: float32 [768, 2304], P(('clip', 'frame'))
- project_out: float32 [768, 768], P(('clip', 'frame')), may hold values from -0.1875 to 0.1875
- expand_weight: float32 [768, 3072], P(('clip', 'frame')), may hold values from -0.21875 to 0.21875
- shrink_weight: float32 [3072, 768], P(('clip', 'frame')), may hold values from -0.15625 to 0.15625
- expand_bias: float32 [3072], P(('clip', 'frame')), may hold values from -3 to 3
- vectors: float32 [768, 8], P(('clip', 'frame'))
- moments_in: float32 [2, 768, 2304], P(None, ('clip', 'frame')), as said below
- moments_out: float32 [2, 768, 768], P(None, ('clip', 'frame'))
- moments_expand: float32 [2, 768, 3072], P(None, ('clip', 'frame'))
- moments_shrink: float32 [2, 3072, 768], P(None, ('clip', 'frame'))
- moments_bias: float32 [2, 3072], P(None, ('clip', 'frame'))
- moments_vectors: float32 [2, 768, 8], P(None, ('clip', 'frame'))
Outputs:
- output: bfloat16 [16, 1500, 768], P('clip', 'frame')
- grad_inputs: bfloat16 [16, 1500, 768], P('clip', 'frame')
- grad_project_in: float32 [768, 2304], P(('clip', 'frame'))
- grad_project_out: float32 [768, 768], P(('clip', 'frame'))
- grad_expand: float32 [768, 3072], P(('clip', 'frame'))
- grad_shrink: float32 [3072, 768], P(('clip', 'frame'))
- grad_bias: float32 [3072], P(('clip', 'frame'))
- grad_vectors: float32 [768, 8], P(('clip', 'frame'))
- new_project_in: float32 [768, 2304], P(('clip', 'frame'))
- new_project_out: float32 [768, 768], P(('clip', 'frame'))
- new_expand: float32 [768, 3072], P(('clip', 'frame'))
- new_shrink: float32 [3072, 768], P(('clip', 'frame'))
- new_bias: float32 [3072], P(('clip', 'frame'))
- new_vectors: float32 [768, 8], P(('clip', 'frame'))
- new_moments_in: float32 [2, 768, 2304], P(None, ('clip', 'frame'))
- new_moments_out: float32 [2, 768, 768], P(None, ('clip', 'frame'))
- new_moments_expand: float32 [2, 768, 3072], P(None, ('clip', 'frame'))
- new_moments_shrink: float32 [2, 3072, 768], P(None, ('clip', 'frame'))
- new_moments_bias: float32 [2, 3072], P(None, ('clip', 'frame'))
- new_moments_vectors: float32 [2, 768, 8], P(None, ('clip', 'frame'))
Inputs may be any that keep to these rules, and one draw needn't show every extreme that they name: `moments_in`: the first row of each moments array is signed, the second positive.
All inputs are finite; a program needn't handle non-finite values.
Results may differ from a plain program's by a relative error of at most 0.013.
The roundings to bfloat16 on the way count: a program that leaves them out, or rounds other values in their place, can miss the bound.
Values may be sent and summed in bfloat16 or wider, within the bound.
A program may use at most 192 MiB of HBM per device.

v0:
```python
import math
import jax
import jax.numpy as jnp
from jax import lax
from jax.sharding import PartitionSpec as P

HEADS = 12
ADAM_STEP = 4
epsilon_norm = 1e-05
beta_first = 0.9
beta_second = 0.99
learn_rate = 0.03
decay_rate = 0.01
epsilon_adam = 1e-08
root_half = 0.7071067811865476
inv_root_two_pi = 0.3989422804014327


def norm_parts(inputs, norm_gain, norm_shift):
    average = jnp.mean(inputs, axis=-1, keepdims=True)
    centered = inputs - average
    spread = jnp.mean(centered * centered, axis=-1, keepdims=True)
    inv_std = lax.rsqrt(spread + epsilon_norm)
    normed = centered * inv_std
    return (normed * norm_gain + norm_shift, normed, inv_std)


def norm_backward(grad_normed, normed, inv_std, norm_gain):
    grad_gain = jnp.sum(grad_normed * normed, axis=0)
    grad_shift = jnp.sum(grad_normed, axis=0)
    scaled = grad_normed * norm_gain
    grad_input = inv_std * (
        scaled
        - jnp.mean(scaled, axis=-1, keepdims=True)
        - normed * jnp.mean(scaled * normed, axis=-1, keepdims=True)
    )
    return (grad_input, grad_gain, grad_shift)


def gelu_exact(inputs):
    return 0.5 * inputs * (1.0 + jax.scipy.special.erf(inputs * root_half))


def gelu_slope(inputs):
    return (
        0.5 * (1.0 + jax.scipy.special.erf(inputs * root_half))
        + inputs * jnp.exp(-0.5 * inputs * inputs) * inv_root_two_pi
    )


def attend_forward(queries, keys_values, head_count):
    model_width = queries.shape[2]
    head_size = model_width // head_count
    score_scale = 1.0 / math.sqrt(head_size)

    def one_head(head_index):
        offset = head_index * head_size
        query_block = lax.dynamic_slice_in_dim(queries, offset, head_size, 2)
        key_block = lax.dynamic_slice_in_dim(keys_values, offset, head_size, 2)
        value_block = lax.dynamic_slice_in_dim(keys_values, model_width + offset, head_size, 2)
        scores = (
            jnp.einsum("cqd,ckd->cqk", query_block, key_block, preferred_element_type=jnp.float32)
            * score_scale
        )
        highest = jnp.max(scores, axis=-1, keepdims=True)
        exponent = jnp.exp(scores - highest)
        denominator = jnp.sum(exponent, axis=-1, keepdims=True)
        weights_soft = (exponent / denominator).astype(jnp.bfloat16)
        mixed = jnp.einsum(
            "cqk,ckd->cqd", weights_soft, value_block, preferred_element_type=jnp.float32
        )
        return (mixed, (highest + jnp.log(denominator))[..., 0])

    mixed, log_totals = lax.map(one_head, jnp.arange(head_count))
    clip_count, frame_count = (queries.shape[0], queries.shape[1])
    mixed = jnp.transpose(mixed, (1, 2, 0, 3)).reshape(clip_count, frame_count, model_width)
    return (mixed, log_totals)


def attend_backward(queries, keys_values, grad_mixed, log_totals, head_count):
    model_width = queries.shape[2]
    head_size = model_width // head_count
    score_scale = 1.0 / math.sqrt(head_size)

    def one_head_back(head_index):
        offset = head_index * head_size
        query_block = lax.dynamic_slice_in_dim(queries, offset, head_size, 2)
        key_block = lax.dynamic_slice_in_dim(keys_values, offset, head_size, 2)
        value_block = lax.dynamic_slice_in_dim(keys_values, model_width + offset, head_size, 2)
        grad_block = lax.dynamic_slice_in_dim(grad_mixed, offset, head_size, 2)
        totals = lax.dynamic_index_in_dim(log_totals, head_index, 0, keepdims=False)
        scores = (
            jnp.einsum("cqd,ckd->cqk", query_block, key_block, preferred_element_type=jnp.float32)
            * score_scale
        )
        weights_soft = jnp.exp(scores - totals[..., None])
        grad_weights = jnp.einsum(
            "cqd,ckd->cqk", grad_block, value_block, preferred_element_type=jnp.float32
        )
        delta = jnp.sum(weights_soft * grad_weights, axis=-1, keepdims=True)
        grad_scores = (weights_soft * (grad_weights - delta)).astype(jnp.bfloat16)
        grad_query = (
            jnp.einsum("cqk,ckd->cqd", grad_scores, key_block, preferred_element_type=jnp.float32)
            * score_scale
        )
        grad_key = (
            jnp.einsum("cqk,cqd->ckd", grad_scores, query_block, preferred_element_type=jnp.float32)
            * score_scale
        )
        grad_value = jnp.einsum(
            "cqk,cqd->ckd",
            weights_soft.astype(jnp.bfloat16),
            grad_block,
            preferred_element_type=jnp.float32,
        )
        return (grad_query, delta[..., 0], grad_key, grad_value)

    pieces = lax.map(one_head_back, jnp.arange(head_count))
    clip_count, frame_count = (queries.shape[0], queries.shape[1])
    clip_frames = keys_values.shape[1]
    grad_query = jnp.transpose(pieces[0], (1, 2, 0, 3)).reshape(
        clip_count, frame_count, model_width
    )
    grad_key = jnp.transpose(pieces[2], (1, 2, 0, 3)).reshape(clip_count, clip_frames, model_width)
    grad_value = jnp.transpose(pieces[3], (1, 2, 0, 3)).reshape(
        clip_count, clip_frames, model_width
    )
    return (grad_query, pieces[1], jnp.concatenate([grad_key, grad_value], axis=2))


def adam_step(weight, moments, gradient):
    first = beta_first * moments[0] + (1.0 - beta_first) * gradient
    second = beta_second * moments[1] + (1.0 - beta_second) * gradient * gradient
    first_hat = first / (1.0 - beta_first**ADAM_STEP)
    second_hat = second / (1.0 - beta_second**ADAM_STEP)
    change = -learn_rate * (first_hat / (jnp.sqrt(second_hat) + epsilon_adam) + decay_rate * weight)
    return (change, jnp.stack([first, second]))


def body(
    inputs,
    cotangent,
    project_in,
    project_out,
    expand_weight,
    shrink_weight,
    expand_bias,
    vectors,
    moments_in,
    moments_out,
    moments_expand,
    moments_shrink,
    moments_bias,
    moments_vectors,
):
    clip_count, frame_count, model_width = inputs.shape
    row_count = clip_count * frame_count
    head_count = HEADS
    shard_rows = project_in.shape[0]
    wide_in = project_in.shape[1]
    ff_width = expand_weight.shape[1]
    swap = [(0, 1), (1, 0)]
    everyone = ("clip", "frame")
    small = jnp.concatenate(
        [
            vectors,
            expand_bias.reshape(shard_rows, -1),
            jnp.zeros(
                (shard_rows, 128 - vectors.shape[1] - expand_bias.shape[0] // shard_rows),
                jnp.float32,
            ),
        ],
        axis=1,
    )
    first_pack = jnp.concatenate([project_in, small], axis=1).astype(jnp.bfloat16)
    second_pack = jnp.concatenate(
        [project_out, expand_weight, shrink_weight.reshape(shard_rows, -1)], axis=1
    ).astype(jnp.bfloat16)
    first_full = lax.all_gather(first_pack, everyone, axis=0, tiled=True)
    second_full = lax.all_gather(second_pack, everyone, axis=0, tiled=True)
    full_in = first_full[:, :wide_in]
    small_full = first_full[:, wide_in:].astype(jnp.float32)
    column_set = small_full[:, : vectors.shape[1]]
    full_bias = small_full[
        :, vectors.shape[1] : vectors.shape[1] + ff_width // model_width
    ].reshape(-1)
    full_out = second_full[:, :model_width]
    full_expand = second_full[:, model_width : model_width + ff_width]
    full_shrink = second_full[:, model_width + ff_width :].reshape(ff_width, model_width)
    frames_rows = inputs.reshape(row_count, model_width).astype(jnp.float32)
    normed_first, plain_first, inv_first = norm_parts(
        frames_rows, column_set[:, 0], column_set[:, 1]
    )
    hidden_first = normed_first.astype(jnp.bfloat16)
    hidden_partner = lax.ppermute(hidden_first, "frame", swap)
    bias_in = jnp.concatenate(
        [column_set[:, 2], jnp.zeros((model_width,), jnp.float32), column_set[:, 3]]
    )
    projected = (
        jnp.dot(hidden_first, full_in, preferred_element_type=jnp.float32) + bias_in
    ).astype(jnp.bfloat16)
    partner_pairs = (
        jnp.dot(hidden_partner, full_in[:, model_width:], preferred_element_type=jnp.float32)
        + bias_in[model_width:]
    ).astype(jnp.bfloat16)
    queries = projected[:, :model_width].reshape(clip_count, frame_count, model_width)
    clip_pairs = jnp.concatenate([projected[:, model_width:], partner_pairs], axis=0).reshape(
        clip_count, 2 * frame_count, 2 * model_width
    )
    mixed, log_totals = attend_forward(queries, clip_pairs, head_count)
    mixed_low = mixed.reshape(row_count, model_width).astype(jnp.bfloat16)
    attended = jnp.dot(mixed_low, full_out, preferred_element_type=jnp.float32) + column_set[:, 4]
    residual = frames_rows + attended
    normed_second, plain_second, inv_second = norm_parts(
        residual, column_set[:, 5], column_set[:, 6]
    )
    hidden_second = normed_second.astype(jnp.bfloat16)
    preact = jnp.dot(hidden_second, full_expand, preferred_element_type=jnp.float32) + full_bias
    activated = gelu_exact(preact).astype(jnp.bfloat16)
    result = (
        residual
        + jnp.dot(activated, full_shrink, preferred_element_type=jnp.float32)
        + column_set[:, 7]
    )
    output = result.astype(jnp.bfloat16).reshape(inputs.shape)
    grad_result = cotangent.reshape(row_count, model_width)
    grad_shrink_term = jnp.dot(activated.T, grad_result, preferred_element_type=jnp.float32)
    grad_down_bias = jnp.sum(grad_result.astype(jnp.float32), axis=0)
    grad_activated = jnp.dot(grad_result, full_shrink.T, preferred_element_type=jnp.float32)
    grad_preact = (grad_activated * gelu_slope(preact)).astype(jnp.bfloat16)
    grad_expand_term = jnp.dot(hidden_second.T, grad_preact, preferred_element_type=jnp.float32)
    grad_bias_term = jnp.sum(grad_preact.astype(jnp.float32), axis=0)
    grad_hidden_second = jnp.dot(grad_preact, full_expand.T, preferred_element_type=jnp.float32)
    norm_term_second, gain_second, shift_second = norm_backward(
        grad_hidden_second, plain_second, inv_second, column_set[:, 5]
    )
    grad_residual = grad_result.astype(jnp.float32) + norm_term_second
    grad_attended = grad_residual.astype(jnp.bfloat16)
    grad_out_term = jnp.dot(mixed_low.T, grad_attended, preferred_element_type=jnp.float32)
    grad_out_bias = jnp.sum(grad_attended.astype(jnp.float32), axis=0)
    owned_late = lax.psum_scatter(
        jnp.concatenate(
            [grad_shrink_term.reshape(model_width, -1), grad_expand_term, grad_out_term], axis=1
        ),
        everyone,
        scatter_dimension=0,
        tiled=True,
    )
    grad_mixed = jnp.dot(grad_attended, full_out.T, preferred_element_type=jnp.float32).astype(
        jnp.bfloat16
    )
    grad_mixed = grad_mixed.reshape(clip_count, frame_count, model_width)
    grad_query, delta_rows, grad_pairs_terms = attend_backward(
        queries, clip_pairs, grad_mixed, log_totals, head_count
    )
    partner_terms = grad_pairs_terms[:, frame_count:].astype(jnp.bfloat16)
    returned_terms = lax.ppermute(partner_terms, "frame", swap)
    grad_pairs = grad_pairs_terms[:, :frame_count] + returned_terms.astype(jnp.float32)
    grad_projected = (
        jnp.concatenate([grad_query, grad_pairs], axis=2)
        .reshape(row_count, 3 * model_width)
        .astype(jnp.bfloat16)
    )
    grad_in_term = jnp.dot(hidden_first.T, grad_projected, preferred_element_type=jnp.float32)
    projected_sums = jnp.sum(grad_projected.astype(jnp.float32), axis=0)
    grad_query_bias = projected_sums[:model_width]
    grad_value_bias = projected_sums[2 * model_width :]
    grad_hidden_first = jnp.dot(grad_projected, full_in.T, preferred_element_type=jnp.float32)
    norm_term_first, gain_first, shift_first = norm_backward(
        grad_hidden_first, plain_first, inv_first, column_set[:, 0]
    )
    grad_inputs = (grad_residual + norm_term_first).astype(jnp.bfloat16).reshape(inputs.shape)
    grad_columns = jnp.stack(
        [
            gain_first,
            shift_first,
            grad_query_bias,
            grad_value_bias,
            grad_out_bias,
            gain_second,
            shift_second,
            grad_down_bias,
        ],
        axis=1,
    )
    small_grads = jnp.concatenate(
        [
            grad_columns,
            grad_bias_term.reshape(model_width, -1),
            jnp.zeros((model_width, 256 - 12), jnp.float32),
        ],
        axis=1,
    )
    first_terms, owned_late = lax.optimization_barrier(
        (jnp.concatenate([grad_in_term, small_grads], axis=1), owned_late)
    )
    owned_first = lax.psum_scatter(first_terms, everyone, scatter_dimension=0, tiled=True)
    owned_in = owned_first[:, :wide_in]
    owned_vectors = owned_first[:, wide_in : wide_in + vectors.shape[1]]
    owned_bias = owned_first[:, wide_in + vectors.shape[1] : wide_in + 12].reshape(-1)
    owned_shrink = owned_late[:, :ff_width].reshape(shrink_weight.shape)
    owned_expand = owned_late[:, ff_width : 2 * ff_width]
    owned_out = owned_late[:, 2 * ff_width :]
    new_in, mom_in = adam_step(project_in, moments_in, owned_in)
    new_out, mom_out = adam_step(project_out, moments_out, owned_out)
    new_expand, mom_expand = adam_step(expand_weight, moments_expand, owned_expand)
    new_shrink, mom_shrink = adam_step(shrink_weight, moments_shrink, owned_shrink)
    new_bias, mom_bias = adam_step(expand_bias, moments_bias, owned_bias)
    new_vectors, mom_vectors = adam_step(vectors, moments_vectors, owned_vectors)
    return (
        output,
        grad_inputs,
        owned_in,
        owned_out,
        owned_expand,
        owned_shrink,
        owned_bias,
        owned_vectors,
        new_in,
        new_out,
        new_expand,
        new_shrink,
        new_bias,
        new_vectors,
        mom_in,
        mom_out,
        mom_expand,
        mom_shrink,
        mom_bias,
        mom_vectors,
    )


def solution(mesh):
    in_specs = (
        P("clip", "frame", None),
        P("clip", "frame", None),
        P(("clip", "frame"), None),
        P(("clip", "frame"), None),
        P(("clip", "frame"), None),
        P(("clip", "frame"), None),
        P(("clip", "frame")),
        P(("clip", "frame"), None),
        P(None, ("clip", "frame"), None),
        P(None, ("clip", "frame"), None),
        P(None, ("clip", "frame"), None),
        P(None, ("clip", "frame"), None),
        P(None, ("clip", "frame")),
        P(None, ("clip", "frame"), None),
    )
    out_specs = (
        P("clip", "frame", None),
        P("clip", "frame", None),
        P(("clip", "frame"), None),
        P(("clip", "frame"), None),
        P(("clip", "frame"), None),
        P(("clip", "frame"), None),
        P(("clip", "frame")),
        P(("clip", "frame"), None),
        P(("clip", "frame"), None),
        P(("clip", "frame"), None),
        P(("clip", "frame"), None),
        P(("clip", "frame"), None),
        P(("clip", "frame")),
        P(("clip", "frame"), None),
        P(None, ("clip", "frame"), None),
        P(None, ("clip", "frame"), None),
        P(None, ("clip", "frame"), None),
        P(None, ("clip", "frame"), None),
        P(None, ("clip", "frame")),
        P(None, ("clip", "frame"), None),
    )
    return jax.shard_map(body, mesh=mesh, in_specs=in_specs, out_specs=out_specs, check_vma=False)
```

profile of v0, /device:TPU:0, one launch (start us, length us, event | category | flops | bytes accessed | tf_op | source)
XLA Modules:
  0.0 796.1 jit_solution(1115466514428548295)
XLA Ops:
  14.4 60.6 %all-gather.3.cloned.1.call-done = bf16[768,2432]{1,0:T(8,128)(2,1)} async-done(((bf16[24,2432]{1,0:T(8,128)(2,1)}), bf16[768,2432]{1,0:T(8,128)(2,1)}) %all-gather.3.cloned.1.call-update) | async-done | bytes 3735568 | tf_op jit(solution)/shard_map/all_gather | solution.py:179
  81.1 5.1 add_convert_fusion
  89.6 18.6 %collective-permute-done = bf16[750,768]{1,0:T(8,128)(2,1)} collective-permute-done((bf16[750,768]{1,0:T(8,128)(2,1)S(1)}, bf16[750,768]{1,0:T(8,128)(2,1)}, u32[]{:S(2)}, u32[]{:S(2)}) %collective-permute-start) | collective-permute-done | bytes 1152032 | tf_op jit(solution)/shard_map/ppermute | solution.py:195
  116.1 126.1 %while.30 = (s32[]{:T(128)}, bf16[12,1,750,64]{2,3,1,0:T(8,128)(2,1)}, f32[12,1,750]{2,1,0:T(1,128)S(1)}, s32[12]{0:T(128)S(1)}, bf16[1,750,768]{2,1,0:T(8,128)(...) while((s32[]{:T(128)}, ...), condition=%wide.region_5.6_spmd, body=%wide.region_2.5_spmd.sunk | while | flops 298124256 | bytes 32810912 | solution.py:74
  154.0 4.5 fusion.160
  246.6 4.8 slice.186
  251.4 8.6 %reshape.414 = bf16[3072,768]{1,0:T(8,128)(2,1)} reshape(bf16[768,3072]{1,0:T(8,128)(2,1)} %slice.186) | data formatting | bytes 9437184 | tf_op jit(solution)/shard_map/reshape | solution.py:189
  260.0 7.1 multiply_convert_fusion.1
  267.1 7.6 convert_reduce_fusion
  274.7 7.0 fusion.127
  281.7 6.7 multiply_reduce_fusion.2
  292.2 6.6 fusion.88
  298.8 11.4 %reshape.423 = f32[768,3072]{1,0:T(8,128)} reshape(f32[3072,768]{1,0:T(8,128)} %fusion.88) | data formatting | bytes 18874368 | tf_op jit(solution)/shard_map/reshape | solution.py:243
  310.3 15.0 %pad_maximum_fusion = f32[768,6912]{1,0:T(8,128)} fusion(f32[768,768]{1,0:T(8,128)} %fusion.124, f32[768,3072]{1,0:T(8,128)} %fusion.127, f32[768,3072]{1,0:T(8,128)} %reshape.423), kind=kLoop, calls=%fused_computation.52 | loop fusion | flops 10616832 | bytes 42467328 | tf_op jit(solution)/shard_map/concatenate | solution.py:242
  330.6 231.7 %while.31 = (s32[]{:T(128)}, bf16[12,1,750,64]{2,3,1,0:T(8,128)(2,1)}, f32[12,1,1500,64]{2,3,1,0:T(8,128)}, f32[12,1,1500,64]{2,3,1,0:T(8,128)}, s32[12]{0:T(128...) while((s32[]{:T(128)}, ...), condition=%wide.region_12.13_spmd, body=%wide.region_10.12_spmd.sunk | while | flops 729143232 | bytes 50654712 | solution.py:118
  338.0 4.5 multiply_reduce_fusion.10
  357.9 4.5 multiply_reduce_fusion.10
  562.3 5.0 fusion.49
  578.5 45.8 %collective-permute-done.1 = bf16[1,750,1536]{2,1,0:T(8,128)(2,1)} collective-permute-done((bf16[1,750,1536]{2,1,0:T(8,128)(2,1)}, bf16[1,750,1536]{2,1,0:T(8,128)(2,1)}, u32[]{:S(2)}, u32[]{:S(2)}) %collective-permute-start.1) | collective-permute-done | bytes 2304032 | tf_op jit(solution)/shard_map/ppermute | solution.py:257
  633.4 4.8 fusion.77
  642.5 6.3 fusion.54
  649.7 10.7 %concatenate.50 = f32[768,2560]{1,0:T(8,128)} concatenate(f32[768,2304]{1,0:T(8,128)} %fusion.54, f32[768,1]{1,0:T(8,128)} %stack.92, f32[768,1]{1,0:T(8,128)} %stack.93, f32[768,1]{1,0:T(8,128)} %stack.94, f32[768,1]{1,0:T(8,128)} %stack.95, f32[768,1]{1,0:T(8,128)} %stack.96, f32[768,1]{1,0:T(8,128)} %stack.97, f32[768,1]{1,0:T(8,128)} %stack.98, f32[768,1]{1,0:T(8,128)} %stack.99, ...), dimensions={1} | concatenate | bytes 15728640 | tf_op jit(solution)/shard_map/concatenate | solution.py:295
  661.4 8.8 %fusion.84 = bf16[1,750,768]{2,1,0:T(8,128)(2,1)} fusion(f32[750,768]{1,0:T(8,128)S(1)} %get-tuple-element.381, bf16[750,3072]{1,0:T(8,128)(2,1)} %copy-done.39, bf16[3072,768]{1,0:T(8,128)(2,1)} %reshape.414, f32[768]{0:T(1024)S(1)} %copy-done.35), kind=kOutput, calls=%fused_computation.124 | convolution fusion | flops 3540672000 | bytes 12785664 | tf_op jit(solution)/shard_map/dot_general | solution.py:222
  679.0 102.6 %reduce-scatter.5.cloned.1.call-done = f32[24,2560]{1,0:T(8,128)} async-done(((f32[768,2560]{1,0:T(8,128)}), f32[24,2560]{1,0:T(8,128)}) %reduce-scatter.5.cloned.1.call-update) | async-done | bytes 245776 | tf_op jit(solution)/shard_map/reduce_scatter | solution.py:297
  (431 shorter events, 384.1 us)
Async XLA Ops:
  7.2 6.4 copy-start.1
  7.2 67.7 %all-gather.3.cloned.1.call-start = ((), (), s32[]{:S(2)}) async-start(), calls=%async_computation.2 | async-start | bytes 3852288 | tf_op jit(solution)/shard_map/all_gather | solution.py:179
  10.6 231.7 %all-gather.5.cloned.1.call-start = ((), (), s32[]{:S(2)}) async-start(), calls=%async_computation.3 | async-start | bytes 10948608 | tf_op jit(solution)/shard_map/all_gather | solution.py:180
  13.9 63.7 %copy-start.24 = (f32[750]{0:T(1024)}, f32[750]{0:T(1024)S(1)}, u32[]{:S(2)}) copy-start(f32[750]{0:T(1024)S(1)} %broadcast_multiply_fusion.5) | copy-start | bytes 9004
  14.4 63.7 %copy-start.28 = (f32[750]{0:T(1024)}, f32[750]{0:T(1024)S(1)}, u32[]{:S(2)}) copy-start(f32[750]{0:T(1024)S(1)} %add_rsqrt_fusion.1) | copy-start | bytes 9004
  77.5 8.7 %copy-start.26 = (f32[768]{0:T(1024)}, f32[768]{0:T(1024)S(1)}, u32[]{:S(2)}) copy-start(f32[768]{0:T(1024)S(1)} %get-tuple-element.317) | copy-start | bytes 9220
  78.0 30.2 %collective-permute-start = (bf16[750,768]{1,0:T(8,128)(2,1)S(1)}, bf16[750,768]{1,0:T(8,128)(2,1)}, u32[]{:S(2)}, u32[]{:S(2)}) collective-permute-start(bf16[750,768]{1,0:T(8,128)(2,1)S(1)} %fusion.71), channel_id=1, source_target_pairs={{0,1},{1,0},{2,3},{3,2},{4,5},{5,4},{6,7},{7,6},{8,9},{9,8},{10,11... | collective-permute-start | bytes 3456008 | tf_op jit(solution)/shard_map/ppermute | solution.py:195
  80.3 580.1 %reduce-scatter.3.cloned.1.call-start = ((), (), s32[]{:S(2)}) async-start(), calls=%async_computation.4 | async-start | bytes 21897216 | tf_op jit(solution)/shard_map/reduce_scatter | solution.py:241
  89.6 22.6 %slice-start.2 = ((bf16[750,2304]{1,0:T(8,128)(2,1)}), bf16[750,1536]{1,0:T(8,128)(2,1)S(1)}, s32[]{:S(2)}) async-start(bf16[750,2304]{1,0:T(8,128)(2,1)} %copy-done.5), calls=%async_computation.8 | async-start | bytes 4620288 | tf_op jit(solution)/shard_map/slice | solution.py:207
  260.0 7.1 copy-start.6
  260.0 7.1 copy-start.16
  267.1 25.1 %copy-start.39 = (bf16[750,3072]{1,0:T(8,128)(2,1)}, bf16[750,3072]{1,0:T(8,128)(2,1)S(1)}, u32[]{:S(2)}) copy-start(bf16[750,3072]{1,0:T(8,128)(2,1)S(1)} %get-tuple-element.386) | copy-start | bytes 13824004
  325.3 456.2 %reduce-scatter.5.cloned.1.call-start = ((), (), s32[]{:S(2)}) async-start(), calls=%async_computation.5 | async-start | bytes 8110080 | tf_op jit(solution)/shard_map/reduce_scatter | solution.py:297
  357.9 4.8 slice-start.1
  571.7 52.6 %collective-permute-start.1 = (bf16[1,750,1536]{2,1,0:T(8,128)(2,1)}, bf16[1,750,1536]{2,1,0:T(8,128)(2,1)}, u32[]{:S(2)}, u32[]{:S(2)}) collective-permute-start(bf16[1,750,1536]{2,1,0:T(8,128)(2,1)} %copy.80), channel_id=1, source_target_pairs={{0,1},{1,0},{2,3},{3,2},{4,5},{5,4},{6,7},{7,6},{8,9},{9,8},{10,11... | collective-permute-start | bytes 6912008 | tf_op jit(solution)/shard_map/ppermute | solution.py:257
  661.4 8.8 %copy-start.4 = (f32[750,768]{1,0:T(8,128)S(1)}, f32[750,768]{1,0:T(8,128)}, u32[]{:S(2)}) copy-start(f32[750,768]{1,0:T(8,128)} %copy-done.3) | copy-start | bytes 6912004
  661.4 8.8 %copy-start.9 = (f32[750,768]{1,0:T(8,128)S(1)}, f32[750,768]{1,0:T(8,128)}, u32[]{:S(2)}) copy-start(f32[750,768]{1,0:T(8,128)} %get-tuple-element.383) | copy-start | bytes 6912004
  672.1 5.0 copy-start.11
  672.2 4.9 copy-start.15
  676.2 107.7 %copy-start.17 = (f32[2,24,2304]{2,1,0:T(8,128)S(1)}, f32[2,24,2304]{2,1,0:T(8,128)}, u32[]{:S(2)}) copy-start(f32[2,24,2304]{2,1,0:T(8,128)} %param.26) | copy-start | bytes 1327108
  677.1 107.8 %copy-start.19 = (f32[24,2304]{1,0:T(8,128)S(1)}, f32[24,2304]{1,0:T(8,128)}, u32[]{:S(2)}) copy-start(f32[24,2304]{1,0:T(8,128)} %param.20) | copy-start | bytes 663556
  677.1 109.3 %copy-start.36 = (f32[2,96]{1,0:T(2,128)S(1)}, f32[2,96]{1,0:T(2,128)}, u32[]{:S(2)}) copy-start(f32[2,96]{1,0:T(2,128)} %param.30) | copy-start | bytes 2308
  677.2 109.3 %copy-start.38 = (f32[96]{0:T(128)S(1)}, f32[96]{0:T(128)}, u32[]{:S(2)}) copy-start(f32[96]{0:T(128)} %param.24) | copy-start | bytes 1156
  782.4 6.7 copy-start.37
  (58 other events, 181.9 us)
Sparse Core Ops, SparseCore 0:
  11.5 63.4 all-gather.2
  80.5 87.9 all-gather.4
  325.4 219.8 reduce-scatter.2
  660.6 120.8 reduce-scatter.4
where the time goes:
time: 803 us; the launch traced here: 796 us
  matrix products  334 us (42%)
  waiting for transfers between devices  228 us (28%)
  local copies, waits for them, and re-layouts  109 us (14%)
  other arithmetic  66.2 us (8%)
  loops' own time  40.4 us (5%)
  between operations  14.9 us (2%)
    reduce_scatter x1, waiting for transfers between devices, body(): lax.psum_scatter(first_terms, everyone, scatter_dimension=0, tiled=True)  103 us
    all_gather x1, waiting for transfers between devices, body(): first_full = lax.all_gather(first_pack, everyone, axis=0, tiled=True)  60.6 us
    dot_general x12, matrix products, one_head(): jnp.einsum('cqk,ckd->cqd', weights_soft, value_block, preferred_element_t...  51.6 us
    dot_general x12, matrix products, one_head_back(): jnp.einsum('cqd,ckd->cqk', query_block, key_block, preferred_element_type...  50 us
    dot_general x12, matrix products, one_head_back(): jnp.einsum('cqd,ckd->cqk', grad_block, value_block, preferred_element_typ...  49.6 us
    ppermute x1, waiting for transfers between devices, body(): returned_terms = lax.ppermute(partner_terms, 'frame', swap)  45.8 us
    another operation x1, loops' own time, attend_backward(): pieces = lax.map(one_head_back, jnp.arange(head_count))  32.1 us
    dot_general x12, matrix products, one_head_back(): jnp.einsum('cqk,ckd->cqd', grad_scores, key_block, preferred_element_type...  30.7 us
  transfers between devices with their start and end apart: 6, of which 4 were waited for; matrix products, arithmetic and copies ran while one was open for 48% of the time, Pallas kernels for 0%

commit v1 on v0

--- a/solution.py
+++ b/solution.py
@@ -176,8 +176,13 @@
     second_pack = jnp.concatenate(
         [project_out, expand_weight, shrink_weight.reshape(shard_rows, -1)], axis=1
     ).astype(jnp.bfloat16)
-    first_full = lax.all_gather(first_pack, everyone, axis=0, tiled=True)
-    second_full = lax.all_gather(second_pack, everyone, axis=0, tiled=True)
+    first_full, second_full = jnp.split(
+        lax.all_gather(
+            jnp.concatenate([first_pack, second_pack], axis=1), everyone, axis=0, tiled=True
+        ),
+        [first_pack.shape[1]],
+        axis=1,
+    )
     full_in = first_full[:, :wide_in]
     small_full = first_full[:, wide_in:].astype(jnp.float32)
     column_set = small_full[:, : vectors.shape[1]]

time: 803 us -> 838 us (1.044)
  waiting for transfers between devices: 228 us -> 258 us
    all_gather x2 -> x1, waiting for transfers between devices: 60.6 us -> 106 us  [body(): lax.all_gather(jnp.concatenate([first_pack, second_pack], axis=1), everyo...]
    ppermute x1, waiting for transfers between devices: 18.6 us -> 4.34 us  [body(): hidden_partner = lax.ppermute(hidden_first, 'frame', swap)]
  transfers between devices with their start and end apart: 6 -> 5, of which waited for: 4 -> 4; matrix products, arithmetic and copies ran while one was open for 48% -> 35% of each run, Pallas kernels for 0% -> 0%
where the time goes in v1:
time: 838 us; the launch traced here: 826 us
  matrix products  335 us (40%)
  waiting for transfers between devices  258 us (31%)
  local copies, waits for them, and re-layouts  109 us (13%)
  other arithmetic  65.7 us (8%)
  loops' own time  40.6 us (5%)
  between operations  14.7 us (2%)
    all_gather x1, waiting for transfers between devices, body(): lax.all_gather(jnp.concatenate([first_pack, second_pack], axis=1), everyo...  106 us
    reduce_scatter x1, waiting for transfers between devices, body(): lax.psum_scatter(first_terms, everyone, scatter_dimension=0, tiled=True)  102 us
    dot_general x12, matrix products, one_head(): jnp.einsum('cqk,ckd->cqd', weights_soft, value_block, preferred_element_t...  50.8 us
    dot_general x12, matrix products, one_head_back(): jnp.einsum('cqd,ckd->cqk', query_block, key_block, preferred_element_type...  50.2 us
    dot_general x12, matrix products, one_head_back(): jnp.einsum('cqd,ckd->cqk', grad_block, value_block, preferred_element_typ...  48.9 us
    ppermute x1, waiting for transfers between devices, body(): returned_terms = lax.ppermute(partner_terms, 'frame', swap)  45.6 us
    another operation x1, loops' own time, attend_backward(): pieces = lax.map(one_head_back, jnp.arange(head_count))  32.1 us
    dot_general x12, matrix products, one_head_back(): jnp.einsum('cqk,ckd->cqd', grad_scores, key_block, preferred_element_type...  30.7 us
  transfers between devices with their start and end apart: 5, of which 4 were waited for; matrix products, arithmetic and copies ran while one was open for 35% of the time, Pallas kernels for 0%

profile of v1, /device:TPU:0, one launch (start us, length us, event | category | flops | bytes accessed | tf_op | source)
XLA Modules:
  0.0 826.1 jit_solution(16577361078320696941)
XLA Ops:
  14.5 106.1 %all-gather.2.cloned.1.call-done = bf16[768,9344]{1,0:T(8,128)(2,1)} async-done(((bf16[24,9344]{1,0:T(8,128)(2,1)}), bf16[768,9344]{1,0:T(8,128)(2,1)}) %all-gather.2.cloned.1.call-update) | async-done | bytes 14352400 | tf_op jit(solution)/shard_map/all_gather | solution.py:180
  125.5 5.1 add_convert_fusion
  132.6 4.8 slice.191
  137.4 8.5 %reshape.414 = bf16[3072,768]{1,0:T(8,128)(2,1)} reshape(bf16[768,3072]{1,0:T(8,128)(2,1)} %slice.191) | data formatting | bytes 9437184 | tf_op jit(solution)/shard_map/reshape | solution.py:194
  147.2 4.3 collective-permute-done
  159.4 126.5 %while.30 = (s32[]{:T(128)}, bf16[12,1,750,64]{2,3,1,0:T(8,128)(2,1)}, f32[12,1,750]{2,1,0:T(1,128)S(1)}, s32[12]{0:T(128)S(1)}, bf16[1,750,768]{2,1,0:T(8,128)(...) while((s32[]{:T(128)}, ...), condition=%wide.region_5.6_spmd, body=%wide.region_2.5_spmd.sunk | while | flops 298124256 | bytes 32810912 | solution.py:74
  290.3 7.2 multiply_convert_fusion.1
  297.6 7.6 convert_reduce_fusion
  305.2 7.0 fusion.127
  312.2 6.7 multiply_reduce_fusion.2
  323.1 6.4 fusion.88
  329.5 11.5 %reshape.423 = f32[768,3072]{1,0:T(8,128)} reshape(f32[3072,768]{1,0:T(8,128)} %fusion.88) | data formatting | bytes 18874368 | tf_op jit(solution)/shard_map/reshape | solution.py:248
  340.9 15.0 %pad_maximum_fusion = f32[768,6912]{1,0:T(8,128)} fusion(f32[768,768]{1,0:T(8,128)} %fusion.124, f32[768,3072]{1,0:T(8,128)} %fusion.127, f32[768,3072]{1,0:T(8,128)} %reshape.423), kind=kLoop, calls=%fused_computation.52 | loop fusion | flops 10616832 | bytes 42467328 | tf_op jit(solution)/shard_map/concatenate | solution.py:247
  361.2 231.2 %while.31 = (s32[]{:T(128)}, bf16[12,1,750,64]{2,3,1,0:T(8,128)(2,1)}, f32[12,1,1500,64]{2,3,1,0:T(8,128)}, f32[12,1,1500,64]{2,3,1,0:T(8,128)}, s32[12]{0:T(128...) while((s32[]{:T(128)}, ...), condition=%wide.region_12.13_spmd, body=%wide.region_10.12_spmd.sunk | while | flops 729143232 | bytes 50654712 | solution.py:118
  368.6 4.5 multiply_reduce_fusion.10
  388.5 4.5 multiply_reduce_fusion.10
  592.4 5.0 fusion.49
  608.4 45.6 %collective-permute-done.1 = bf16[1,750,1536]{2,1,0:T(8,128)(2,1)} collective-permute-done((bf16[1,750,1536]{2,1,0:T(8,128)(2,1)}, bf16[1,750,1536]{2,1,0:T(8,128)(2,1)}, u32[]{:S(2)}, u32[]{:S(2)}) %collective-permute-start.1) | collective-permute-done | bytes 2304032 | tf_op jit(solution)/shard_map/ppermute | solution.py:262
  654.0 4.4 copy.81
  662.2 6.8 fusion.77
  673.3 6.3 fusion.54
  680.5 10.7 %concatenate.49 = f32[768,2560]{1,0:T(8,128)} concatenate(f32[768,2304]{1,0:T(8,128)} %fusion.54, f32[768,1]{1,0:T(8,128)} %stack.92, f32[768,1]{1,0:T(8,128)} %stack.93, f32[768,1]{1,0:T(8,128)} %stack.94, f32[768,1]{1,0:T(8,128)} %stack.95, f32[768,1]{1,0:T(8,128)} %stack.96, f32[768,1]{1,0:T(8,128)} %stack.97, f32[768,1]{1,0:T(8,128)} %stack.98, f32[768,1]{1,0:T(8,128)} %stack.99, ...), dimensions={1} | concatenate | bytes 15728640 | tf_op jit(solution)/shard_map/concatenate | solution.py:300
  692.1 8.8 %fusion.84 = bf16[1,750,768]{2,1,0:T(8,128)(2,1)} fusion(f32[750,768]{1,0:T(8,128)S(1)} %get-tuple-element.381, bf16[750,3072]{1,0:T(8,128)(2,1)} %copy-done.37, bf16[3072,768]{1,0:T(8,128)(2,1)} %reshape.414, f32[768]{0:T(1024)S(1)} %copy-done.33), kind=kOutput, calls=%fused_computation.124 | convolution fusion | flops 3540672000 | bytes 12785664 | tf_op jit(solution)/shard_map/dot_general | solution.py:227
  709.7 102.1 %reduce-scatter.5.cloned.1.call-done = f32[24,2560]{1,0:T(8,128)} async-done(((f32[768,2560]{1,0:T(8,128)}), f32[24,2560]{1,0:T(8,128)}) %reduce-scatter.5.cloned.1.call-update) | async-done | bytes 245776 | tf_op jit(solution)/shard_map/reduce_scatter | solution.py:302
  (428 shorter events, 381.8 us)
Async XLA Ops:
  7.2 6.5 copy-start.1
  7.2 113.4 %all-gather.2.cloned.1.call-start = ((), (), s32[]{:S(2)}) async-start(), calls=%async_computation.2 | async-start | bytes 14800896 | tf_op jit(solution)/shard_map/all_gather | solution.py:180
  13.7 677.6 %reduce-scatter.3.cloned.1.call-start = ((), (), s32[]{:S(2)}) async-start(), calls=%async_computation.3 | async-start | bytes 21897216 | tf_op jit(solution)/shard_map/reduce_scatter | solution.py:246
  14.0 109.3 %copy-start.23 = (f32[750]{0:T(1024)}, f32[750]{0:T(1024)S(1)}, u32[]{:S(2)}) copy-start(f32[750]{0:T(1024)S(1)} %broadcast_multiply_fusion.5) | copy-start | bytes 9004
  14.5 109.2 %copy-start.27 = (f32[750]{0:T(1024)}, f32[750]{0:T(1024)S(1)}, u32[]{:S(2)}) copy-start(f32[750]{0:T(1024)S(1)} %add_rsqrt_fusion.1) | copy-start | bytes 9004
  123.2 7.4 copy-start.29
  123.7 27.8 %collective-permute-start = (bf16[750,768]{1,0:T(8,128)(2,1)S(1)}, bf16[750,768]{1,0:T(8,128)(2,1)}, u32[]{:S(2)}, u32[]{:S(2)}) collective-permute-start(bf16[750,768]{1,0:T(8,128)(2,1)S(1)} %fusion.71), channel_id=1, source_target_pairs={{0,1},{1,0},{2,3},{3,2},{4,5},{5,4},{6,7},{7,6},{8,9},{9,8},{10,11... | collective-permute-start | bytes 3456008 | tf_op jit(solution)/shard_map/ppermute | solution.py:200
  147.2 8.3 %slice-start.2 = ((bf16[750,2304]{1,0:T(8,128)(2,1)}), bf16[750,1536]{1,0:T(8,128)(2,1)S(1)}, s32[]{:S(2)}) async-start(bf16[750,2304]{1,0:T(8,128)(2,1)} %copy-done.5), calls=%async_computation.7 | async-start | bytes 4620288 | tf_op jit(solution)/shard_map/slice | solution.py:212
  289.9 7.7 slice-start.3
  290.3 7.3 slice-start.4
  290.3 7.3 copy-start.15
  297.5 25.6 %copy-start.37 = (bf16[750,3072]{1,0:T(8,128)(2,1)}, bf16[750,3072]{1,0:T(8,128)(2,1)S(1)}, u32[]{:S(2)}) copy-start(bf16[750,3072]{1,0:T(8,128)(2,1)S(1)} %get-tuple-element.386) | copy-start | bytes 13824004
  356.0 455.9 %reduce-scatter.5.cloned.1.call-start = ((), (), s32[]{:S(2)}) async-start(), calls=%async_computation.4 | async-start | bytes 8110080 | tf_op jit(solution)/shard_map/reduce_scatter | solution.py:302
  368.6 4.8 slice-start.1
  601.8 52.2 %collective-permute-start.1 = (bf16[1,750,1536]{2,1,0:T(8,128)(2,1)}, bf16[1,750,1536]{2,1,0:T(8,128)(2,1)}, u32[]{:S(2)}, u32[]{:S(2)}) collective-permute-start(bf16[1,750,1536]{2,1,0:T(8,128)(2,1)} %copy.80), channel_id=1, source_target_pairs={{0,1},{1,0},{2,3},{3,2},{4,5},{5,4},{6,7},{7,6},{8,9},{9,8},{10,11... | collective-permute-start | bytes 6912008 | tf_op jit(solution)/shard_map/ppermute | solution.py:262
  692.1 8.8 %copy-start.4 = (f32[750,768]{1,0:T(8,128)S(1)}, f32[750,768]{1,0:T(8,128)}, u32[]{:S(2)}) copy-start(f32[750,768]{1,0:T(8,128)} %copy-done.3) | copy-start | bytes 6912004
  692.1 8.8 %copy-start.8 = (f32[750,768]{1,0:T(8,128)S(1)}, f32[750,768]{1,0:T(8,128)}, u32[]{:S(2)}) copy-start(f32[750,768]{1,0:T(8,128)} %get-tuple-element.383) | copy-start | bytes 6912004
  702.9 5.0 copy-start.10
  703.0 4.9 copy-start.14
  707.0 107.3 %copy-start.16 = (f32[2,24,2304]{2,1,0:T(8,128)S(1)}, f32[2,24,2304]{2,1,0:T(8,128)}, u32[]{:S(2)}) copy-start(f32[2,24,2304]{2,1,0:T(8,128)} %param.26) | copy-start | bytes 1327108
  707.9 107.3 %copy-start.18 = (f32[24,2304]{1,0:T(8,128)S(1)}, f32[24,2304]{1,0:T(8,128)}, u32[]{:S(2)}) copy-start(f32[24,2304]{1,0:T(8,128)} %param.20) | copy-start | bytes 663556
  707.9 108.8 %copy-start.34 = (f32[2,96]{1,0:T(2,128)S(1)}, f32[2,96]{1,0:T(2,128)}, u32[]{:S(2)}) copy-start(f32[2,96]{1,0:T(2,128)} %param.30) | copy-start | bytes 2308
  707.9 108.8 %copy-start.36 = (f32[96]{0:T(128)S(1)}, f32[96]{0:T(128)}, u32[]{:S(2)}) copy-start(f32[96]{0:T(128)} %param.24) | copy-start | bytes 1156
  812.7 6.7 copy-start.35
  (57 other events, 177.3 us)
Sparse Core Ops, SparseCore 0:
  13.8 106.7 all-gather.1
  356.1 217.9 reduce-scatter.2
  691.4 120.3 reduce-scatter.4
